TPU v7x, 128 devices: a whole 4x4x4 slice. The times are simulated.
128 devices in a mesh: smp: 8 (over x_lo, z), bld: 16 (over y, x_hi, core).
Axes of the slice: x: 4 (x_hi: 2, x_lo: 2; x = x_hi * 2 + x_lo), y: 4, z: 4, core: 2. Of those that a mesh axis runs over, the one named last changes fastest.
Arguments:
- tensor: bfloat16 [4, 8192, 16384], P(None, 'smp', 'bld'), may hold values from -576 to 576
- building_factor: float32 [64, 16384], P(None, 'bld'), may hold values from -144 to 144
- hour_weights: float32 [4, 64], replicated, may hold values from -5 to 5
Outputs:
- sample_factor: float32 [64, 8192], P(None, ('smp', 'bld'))
- building_out: float32 [64, 16384], P(None, ('bld', 'smp'))
- hour_out: float32 [4, 64], replicated
All inputs are finite; a program needn't handle non-finite values.
Results may differ from a plain program's by a relative error of at most 0.008.
Values may be sent and summed in bfloat16 or wider, within the bound.
A program may use at most 64 MiB of HBM per device.

v0:
```python
import math
import jax
import jax.numpy as jnp
from jax import lax
from jax.sharding import PartitionSpec as P

SWEEPS = 5
EPSILON = 1e-06
RIDGE_SHARE = 0.05


def regularized(gram):
    order_size = gram.shape[0]
    return gram + RIDGE_SHARE * jnp.mean(jnp.diagonal(gram)) * jnp.eye(order_size, dtype=gram.dtype)


def solve_rows(gram, right_side):
    lower_factor = jnp.linalg.cholesky(regularized(gram))
    middle = lax.linalg.triangular_solve(lower_factor, right_side, left_side=True, lower=True)
    return lax.linalg.triangular_solve(
        lower_factor, middle, left_side=True, lower=True, transpose_a=True
    )


def finish(unscaled, gram_raw, row_count):
    column_norm = jnp.sqrt(jnp.diagonal(gram_raw) / row_count + EPSILON)
    return (
        unscaled / column_norm[:, None],
        gram_raw / (column_norm[:, None] * column_norm[None, :]),
    )


def hour_gram(hourly):
    return jnp.dot(hourly.T, hourly, precision=lax.Precision.HIGHEST)


def self_gram(unscaled):
    return jnp.dot(unscaled, unscaled.T, precision=lax.Precision.HIGHEST)


def local(tensor, building_factor, hour_weights):
    samples_total = tensor.shape[1] * lax.axis_size("smp")
    buildings_total = tensor.shape[2] * lax.axis_size("bld")
    scale_up = math.sqrt(samples_total * buildings_total)
    hourly = hour_weights / scale_up
    gram_build = lax.psum(self_gram(building_factor), "bld")
    build_low = building_factor.astype(jnp.bfloat16)
    partial_value = jnp.einsum("rj,kij->kri", build_low, tensor, preferred_element_type=jnp.float32)
    sample_out = None
    building_out = None
    for sweep_index in range(SWEEPS):
        sample_terms = jnp.sum(hourly[:, :, None] * partial_value, axis=0)
        sample_rhs = lax.psum(sample_terms, "bld")
        unscaled = solve_rows(gram_build * hour_gram(hourly), sample_rhs)
        gram_raw = lax.psum(self_gram(unscaled), "smp")
        samples_now, gram_sample = finish(unscaled, gram_raw, samples_total)
        sample_low = samples_now.astype(jnp.bfloat16)
        share_width = samples_now.shape[1] // lax.axis_size("bld")
        sample_out = lax.dynamic_slice_in_dim(
            samples_now, lax.axis_index("bld") * share_width, share_width, 1
        )
        mixed = jnp.einsum("ri,kij->krj", sample_low, tensor, preferred_element_type=jnp.float32)
        build_terms = jnp.sum(hourly[:, :, None] * mixed, axis=0)
        build_rhs = lax.psum(build_terms, "smp")
        unscaled = solve_rows(gram_sample * hour_gram(hourly), build_rhs)
        gram_raw = lax.psum(self_gram(unscaled), "bld")
        building_now, gram_build = finish(unscaled, gram_raw, buildings_total)
        build_low = building_now.astype(jnp.bfloat16)
        share_width = building_now.shape[1] // lax.axis_size("smp")
        building_out = lax.dynamic_slice_in_dim(
            building_now, lax.axis_index("smp") * share_width, share_width, 1
        )
        partial_value = jnp.einsum(
            "rj,kij->kri", build_low, tensor, preferred_element_type=jnp.float32
        )
        hour_terms = jnp.sum(sample_low.astype(jnp.float32)[None, :, :] * partial_value, axis=2)
        hour_rhs = lax.psum(hour_terms, ("smp", "bld"))
        hourly = solve_rows(gram_sample * gram_build, hour_rhs.T).T
    return (sample_out, building_out, hourly * scale_up)


def solution(mesh):
    in_specs = (P(None, "smp", "bld"), P(None, "bld"), P())
    out_specs = (P(None, ("smp", "bld")), P(None, ("bld", "smp")), P())
    return jax.shard_map(local, mesh=mesh, in_specs=in_specs, out_specs=out_specs, check_vma=False)
```

profile of v0, /device:TPU:1, one launch (start us, length us, event | category | flops | bytes accessed | tf_op | source)
XLA Modules:
  0.0 2094.5 jit_solution(17855161390660669668)
XLA Ops:
  8.0 6.7 fusion.10
  15.2 65.3 %psum.182 = f32[64,64]{0,1:T(8,128)S(1)} all-reduce(f32[64,64]{0,1:T(8,128)S(1)} %fusion.159), channel_id=1, replica_groups=mesh['smp'=8,'bld'=16] {'bld'}, use_global_device_ids=true, to_apply=%region_0.0 | all-reduce | flops 4096 | bytes 32768 | tf_op jit(solution)/shard_map/psum | solution.py:46
  82.9 5.8 cholesky.239
  95.0 60.6 %all-reduce.11.cloned.1.call-done = f32[64,1024]{1,0:T(8,128)} async-done(((f32[64,1024]{1,0:T(8,128)}), f32[64,1024]{1,0:T(8,128)}) %all-reduce.11.cloned.1.call-update) | async-done | bytes 262160 | tf_op jit(solution)/shard_map/psum | solution.py:53
  157.7 26.2 %psum.184 = f32[64,64]{0,1:T(8,128)S(1)} all-reduce(f32[64,64]{0,1:T(8,128)S(1)} %fusion.160), channel_id=1, replica_groups=mesh['smp'=8,'bld'=16] {'smp'}, use_global_device_ids=true, to_apply=%region_6.10 | all-reduce | flops 4096 | bytes 32768 | tf_op jit(solution)/shard_map/psum | solution.py:55
  192.8 5.8 cholesky.250
  205.1 65.8 %all-reduce.13.cloned.1.call-done = f32[64,1024]{1,0:T(8,128)} async-done(((f32[64,1024]{1,0:T(8,128)}), f32[64,1024]{1,0:T(8,128)}) %all-reduce.13.cloned.1.call-update) | async-done | bytes 262160 | tf_op jit(solution)/shard_map/psum | solution.py:64
  273.0 65.3 %psum.186 = f32[64,64]{0,1:T(8,128)S(1)} all-reduce(f32[64,64]{0,1:T(8,128)S(1)} %fusion.161), channel_id=1, replica_groups=mesh['smp'=8,'bld'=16] {'bld'}, use_global_device_ids=true, to_apply=%region_10.14 | all-reduce | flops 4096 | bytes 32768 | tf_op jit(solution)/shard_map/psum | solution.py:66
  341.4 5.8 cholesky.261
  353.5 6.2 multiply_reduce_fusion.7
  359.6 67.3 %psum.187 = f32[64,4]{0,1:T(4,128)S(1)} all-reduce(f32[64,4]{0,1:T(4,128)S(1)} %bitcast.367), channel_id=1, replica_groups=mesh['smp'=8,'bld'=16] {'smp','bld'}, use_global_device_ids=true, to_apply=%region_13.17 | all-reduce | flops 256 | bytes 2048 | tf_op jit(solution)/shard_map/psum | solution.py:77
  429.7 5.8 cholesky.272
  442.7 127.8 %all-reduce.15.cloned.1.call-done = f32[64,1024]{1,0:T(8,128)} async-done(((f32[64,1024]{1,0:T(8,128)}), f32[64,1024]{1,0:T(8,128)}) %all-reduce.15.cloned.1.call-update) | async-done | bytes 262160 | tf_op jit(solution)/shard_map/psum | solution.py:53
  572.6 26.5 %psum.189 = f32[64,64]{0,1:T(8,128)S(1)} all-reduce(f32[64,64]{0,1:T(8,128)S(1)} %fusion.162), channel_id=1, replica_groups=mesh['smp'=8,'bld'=16] {'smp'}, use_global_device_ids=true, to_apply=%region_17.23 | all-reduce | flops 4096 | bytes 32768 | tf_op jit(solution)/shard_map/psum | solution.py:55
  607.9 5.8 cholesky.283
  620.2 65.8 %all-reduce.17.cloned.1.call-done = f32[64,1024]{1,0:T(8,128)} async-done(((f32[64,1024]{1,0:T(8,128)}), f32[64,1024]{1,0:T(8,128)}) %all-reduce.17.cloned.1.call-update) | async-done | bytes 262160 | tf_op jit(solution)/shard_map/psum | solution.py:64
  688.1 64.7 %psum.191 = f32[64,64]{0,1:T(8,128)S(1)} all-reduce(f32[64,64]{0,1:T(8,128)S(1)} %fusion.163), channel_id=1, replica_groups=mesh['smp'=8,'bld'=16] {'bld'}, use_global_device_ids=true, to_apply=%region_21.27 | all-reduce | flops 4096 | bytes 32768 | tf_op jit(solution)/shard_map/psum | solution.py:66
  755.9 5.8 cholesky.294
  768.0 6.2 multiply_reduce_fusion.5
  774.2 67.5 %psum.192 = f32[64,4]{0,1:T(4,128)S(1)} all-reduce(f32[64,4]{0,1:T(4,128)S(1)} %bitcast.368), channel_id=1, replica_groups=mesh['smp'=8,'bld'=16] {'smp','bld'}, use_global_device_ids=true, to_apply=%region_24.30 | all-reduce | flops 256 | bytes 2048 | tf_op jit(solution)/shard_map/psum | solution.py:77
  844.5 5.8 cholesky.305
  857.5 127.8 %all-reduce.19.cloned.1.call-done = f32[64,1024]{1,0:T(8,128)} async-done(((f32[64,1024]{1,0:T(8,128)}), f32[64,1024]{1,0:T(8,128)}) %all-reduce.19.cloned.1.call-update) | async-done | bytes 262160 | tf_op jit(solution)/shard_map/psum | solution.py:53
  987.4 26.2 %psum.194 = f32[64,64]{0,1:T(8,128)S(1)} all-reduce(f32[64,64]{0,1:T(8,128)S(1)} %fusion.164), channel_id=1, replica_groups=mesh['smp'=8,'bld'=16] {'smp'}, use_global_device_ids=true, to_apply=%region_28.34 | all-reduce | flops 4096 | bytes 32768 | tf_op jit(solution)/shard_map/psum | solution.py:55
  1022.4 5.8 cholesky.316
  1034.7 65.8 %all-reduce.21.cloned.1.call-done = f32[64,1024]{1,0:T(8,128)} async-done(((f32[64,1024]{1,0:T(8,128)}), f32[64,1024]{1,0:T(8,128)}) %all-reduce.21.cloned.1.call-update) | async-done | bytes 262160 | tf_op jit(solution)/shard_map/psum | solution.py:64
  1102.6 65.2 %psum.196 = f32[64,64]{0,1:T(8,128)S(1)} all-reduce(f32[64,64]{0,1:T(8,128)S(1)} %fusion.165), channel_id=1, replica_groups=mesh['smp'=8,'bld'=16] {'bld'}, use_global_device_ids=true, to_apply=%region_32.38 | all-reduce | flops 4096 | bytes 32768 | tf_op jit(solution)/shard_map/psum | solution.py:66
  1170.8 5.8 cholesky.327
  1182.9 6.2 multiply_reduce_fusion.3
  1189.1 67.3 %psum.197 = f32[64,4]{0,1:T(4,128)S(1)} all-reduce(f32[64,4]{0,1:T(4,128)S(1)} %bitcast.369), channel_id=1, replica_groups=mesh['smp'=8,'bld'=16] {'smp','bld'}, use_global_device_ids=true, to_apply=%region_35.41 | all-reduce | flops 256 | bytes 2048 | tf_op jit(solution)/shard_map/psum | solution.py:77
  1259.2 5.8 cholesky.338
  1272.2 127.8 %all-reduce.23.cloned.1.call-done = f32[64,1024]{1,0:T(8,128)} async-done(((f32[64,1024]{1,0:T(8,128)}), f32[64,1024]{1,0:T(8,128)}) %all-reduce.23.cloned.1.call-update) | async-done | bytes 262160 | tf_op jit(solution)/shard_map/psum | solution.py:53
  1402.0 26.5 %psum.199 = f32[64,64]{0,1:T(8,128)S(1)} all-reduce(f32[64,64]{0,1:T(8,128)S(1)} %fusion.166), channel_id=1, replica_groups=mesh['smp'=8,'bld'=16] {'smp'}, use_global_device_ids=true, to_apply=%region_39.45 | all-reduce | flops 4096 | bytes 32768 | tf_op jit(solution)/shard_map/psum | solution.py:55
  1429.4 5.8 fusion.8
  1437.4 5.8 cholesky.349
  1449.7 65.8 %all-reduce.25.cloned.1.call-done = f32[64,1024]{1,0:T(8,128)} async-done(((f32[64,1024]{1,0:T(8,128)}), f32[64,1024]{1,0:T(8,128)}) %all-reduce.25.cloned.1.call-update) | async-done | bytes 262160 | tf_op jit(solution)/shard_map/psum | solution.py:64
  1517.6 64.7 %psum.201 = f32[64,64]{0,1:T(8,128)S(1)} all-reduce(f32[64,64]{0,1:T(8,128)S(1)} %fusion.167), channel_id=1, replica_groups=mesh['smp'=8,'bld'=16] {'bld'}, use_global_device_ids=true, to_apply=%region_43.49 | all-reduce | flops 4096 | bytes 32768 | tf_op jit(solution)/shard_map/psum | solution.py:66
  1585.4 5.8 cholesky.360
  1597.5 6.2 multiply_reduce_fusion.1
  1603.6 67.5 %psum.202 = f32[64,4]{0,1:T(4,128)S(1)} all-reduce(f32[64,4]{0,1:T(4,128)S(1)} %bitcast.370), channel_id=1, replica_groups=mesh['smp'=8,'bld'=16] {'smp','bld'}, use_global_device_ids=true, to_apply=%region_46.52 | all-reduce | flops 256 | bytes 2048 | tf_op jit(solution)/shard_map/psum | solution.py:77
  1673.9 5.8 cholesky.371
  1686.9 127.8 %all-reduce.27.cloned.1.call-done = f32[64,1024]{1,0:T(8,128)} async-done(((f32[64,1024]{1,0:T(8,128)}), f32[64,1024]{1,0:T(8,128)}) %all-reduce.27.cloned.1.call-update) | async-done | bytes 262160 | tf_op jit(solution)/shard_map/psum | solution.py:53
  1816.8 26.2 %psum.204 = f32[64,64]{0,1:T(8,128)S(1)} all-reduce(f32[64,64]{0,1:T(8,128)S(1)} %fusion.168), channel_id=1, replica_groups=mesh['smp'=8,'bld'=16] {'smp'}, use_global_device_ids=true, to_apply=%region_50.56 | all-reduce | flops 4096 | bytes 32768 | tf_op jit(solution)/shard_map/psum | solution.py:55
  1846.2 5.8 cholesky.382
  1864.7 65.3 %all-reduce.29.cloned.1.call-done = f32[64,1024]{1,0:T(8,128)} async-done(((f32[64,1024]{1,0:T(8,128)}), f32[64,1024]{1,0:T(8,128)}) %all-reduce.29.cloned.1.call-update) | async-done | bytes 262160 | tf_op jit(solution)/shard_map/psum | solution.py:64
  1932.1 65.0 %psum.206 = f32[64,64]{0,1:T(8,128)S(1)} all-reduce(f32[64,64]{0,1:T(8,128)S(1)} %fusion.169), channel_id=1, replica_groups=mesh['smp'=8,'bld'=16] {'bld'}, use_global_device_ids=true, to_apply=%region_54.60 | all-reduce | flops 4096 | bytes 32768 | tf_op jit(solution)/shard_map/psum | solution.py:66
  2000.3 5.8 cholesky.393
  2012.4 6.2 fusion.11
  2018.5 67.3 %psum.207 = f32[64,4]{0,1:T(4,128)S(1)} all-reduce(f32[64,4]{0,1:T(4,128)S(1)} %fusion.11), channel_id=1, replica_groups=mesh['smp'=8,'bld'=16] {'smp','bld'}, use_global_device_ids=true, to_apply=%region_57.63 | all-reduce | flops 256 | bytes 2048 | tf_op jit(solution)/shard_map/psum | solution.py:77
  (253 shorter events, 179.2 us)
Async XLA Ops:
  7.2 73.3 %copy-start.1 = (f32[4,64]{1,0:T(4,128)S(1)}, f32[4,64]{1,0:T(4,128)}, u32[]{:S(2)}) copy-start(f32[4,64]{1,0:T(4,128)} %param.14) | copy-start | bytes 3076
  7.2 7.6 copy-start
  7.2 148.4 %all-reduce.11.cloned.1.call-start = ((), (), s32[]{:S(2)}) async-start(), calls=%async_computation | async-start | bytes 524288 | tf_op jit(solution)/shard_map/psum | solution.py:53
  14.7 256.2 %all-reduce.13.cloned.1.call-start = ((), (), s32[]{:S(2)}) async-start(), calls=%async_computation.1 | async-start | bytes 524288 | tf_op jit(solution)/shard_map/psum | solution.py:64
  199.4 371.1 %all-reduce.15.cloned.1.call-start = ((), (), s32[]{:S(2)}) async-start(), calls=%async_computation.2 | async-start | bytes 524288 | tf_op jit(solution)/shard_map/psum | solution.py:53
  436.5 249.5 %all-reduce.17.cloned.1.call-start = ((), (), s32[]{:S(2)}) async-start(), calls=%async_computation.3 | async-start | bytes 524288 | tf_op jit(solution)/shard_map/psum | solution.py:64
  614.5 370.8 %all-reduce.19.cloned.1.call-start = ((), (), s32[]{:S(2)}) async-start(), calls=%async_computation.4 | async-start | bytes 524288 | tf_op jit(solution)/shard_map/psum | solution.py:53
  851.2 249.2 %all-reduce.21.cloned.1.call-start = ((), (), s32[]{:S(2)}) async-start(), calls=%async_computation.5 | async-start | bytes 524288 | tf_op jit(solution)/shard_map/psum | solution.py:64
  1029.0 371.0 %all-reduce.23.cloned.1.call-start = ((), (), s32[]{:S(2)}) async-start(), calls=%async_computation.6 | async-start | bytes 524288 | tf_op jit(solution)/shard_map/psum | solution.py:53
  1265.9 249.5 %all-reduce.25.cloned.1.call-start = ((), (), s32[]{:S(2)}) async-start(), calls=%async_computation.7 | async-start | bytes 524288 | tf_op jit(solution)/shard_map/psum | solution.py:64
  1443.9 370.8 %all-reduce.27.cloned.1.call-start = ((), (), s32[]{:S(2)}) async-start(), calls=%async_computation.8 | async-start | bytes 524288 | tf_op jit(solution)/shard_map/psum | solution.py:53
  1680.7 249.3 %all-reduce.29.cloned.1.call-start = ((), (), s32[]{:S(2)}) async-start(), calls=%async_computation.9 | async-start | bytes 524288 | tf_op jit(solution)/shard_map/psum | solution.py:64
Sparse Core Ops, SparseCore 0:
  14.8 140.7 all-reduce.10
  199.5 71.3 all-reduce.12
  436.6 133.8 all-reduce.14
  614.6 71.3 all-reduce.16
  851.4 133.8 all-reduce.18
  1029.1 71.3 all-reduce.20
  1266.0 133.8 all-reduce.22
  1444.1 71.3 all-reduce.24
  1680.8 133.8 all-reduce.26
  1858.6 71.3 all-reduce.28
where the time goes:
time: 2100 us; the launch traced here: 2090 us
  waiting for transfers between devices  900 us (43%)
  blocking collectives  859 us (41%)
  other arithmetic  196 us (9%)
  matrix products  90.9 us (4%)
  between operations  25.1 us (1%)
  local copies, waits for them, and re-layouts  22.6 us (1%)
    psum x5, waiting for transfers between devices, local(): sample_rhs = lax.psum(sample_terms, 'bld')  572 us
    psum x5, blocking collectives, local(): hour_rhs = lax.psum(hour_terms, ('smp', 'bld'))  337 us
    psum x5, waiting for transfers between devices, local(): build_rhs = lax.psum(build_terms, 'smp')  328 us
    psum x5, blocking collectives, local(): gram_raw = lax.psum(self_gram(unscaled), 'bld')  325 us
    psum x5, blocking collectives, local(): gram_raw = lax.psum(self_gram(unscaled), 'smp')  132 us
    another operation x45, other arithmetic, solve_rows(): lower_factor = jnp.linalg.cholesky(regularized(gram))  97.7 us
    another operation x30, other arithmetic, solve_rows(): lax.linalg.triangular_solve(lower_factor, middle, left_side=True, lower=T...  83.3 us
    psum x1, blocking collectives, local(): gram_build = lax.psum(self_gram(building_factor), 'bld')  65.3 us
  transfers between devices with their start and end apart: 10, of which 10 were waited for; matrix products, arithmetic and copies ran while one was open for 3% of the time, Pallas kernels for 0%

commit v1 on v0

--- a/solution.py
+++ b/solution.py
@@ -74,7 +74,7 @@
             "rj,kij->kri", build_low, tensor, preferred_element_type=jnp.float32
         )
         hour_terms = jnp.sum(sample_low.astype(jnp.float32)[None, :, :] * partial_value, axis=2)
-        hour_rhs = lax.psum(hour_terms, ("smp", "bld"))
+        hour_rhs = jnp.sum(lax.all_gather(hour_terms, ("smp", "bld")), axis=0)
         hourly = solve_rows(gram_sample * gram_build, hour_rhs.T).T
     return (sample_out, building_out, hourly * scale_up)
 

time: 2100 us -> 2650 us (1.26)
  blocking collectives: 859 us -> 1410 us
    all_gather x0 -> x5, blocking collectives: none -> 883 us  [local(): hour_rhs = jnp.sum(lax.all_gather(hour_terms, ('smp', 'bld')), axis=0)]
    psum x5 -> x0, blocking collectives: 337 us -> none  [local(): hour_rhs = lax.psum(hour_terms, ('smp', 'bld'))]
where the time goes in v1:
time: 2650 us; the launch traced here: 2640 us
  blocking collectives  1410 us (53%)
  waiting for transfers between devices  899 us (34%)
  other arithmetic  197 us (7%)
  matrix products  90.9 us (3%)
    all_gather x5, blocking collectives, local(): hour_rhs = jnp.sum(lax.all_gather(hour_terms, ('smp', 'bld')), axis=0)  883 us
    psum x5, waiting for transfers between devices, local(): sample_rhs = lax.psum(sample_terms, 'bld')  571 us
    psum x5, waiting for transfers between devices, local(): build_rhs = lax.psum(build_terms, 'smp')  328 us
    psum x5, blocking collectives, local(): gram_raw = lax.psum(self_gram(unscaled), 'bld')  324 us
    psum x5, blocking collectives, local(): gram_raw = lax.psum(self_gram(unscaled), 'smp')  132 us
    another operation x45, other arithmetic, solve_rows(): lower_factor = jnp.linalg.cholesky(regularized(gram))  97.7 us
    another operation x30, other arithmetic, solve_rows(): lax.linalg.triangular_solve(lower_factor, middle, left_side=True, lower=T...  83.3 us
    psum x1, blocking collectives, local(): gram_build = lax.psum(self_gram(building_factor), 'bld')  65.3 us
  transfers between devices with their start and end apart: 10, of which 10 were waited for; matrix products, arithmetic and copies ran while one was open for 3% of the time, Pallas kernels for 0%

profile of v1, /device:TPU:1, one launch (start us, length us, event | category | flops | bytes accessed | tf_op | source)
XLA Modules:
  0.0 2640.6 jit_solution(9617583012744075826)
XLA Ops:
  8.0 6.8 fusion.10
  15.2 65.3 %psum.147 = f32[64,64]{0,1:T(8,128)S(1)} all-reduce(f32[64,64]{0,1:T(8,128)S(1)} %fusion.164), channel_id=1, replica_groups=mesh['smp'=8,'bld'=16] {'bld'}, use_global_device_ids=true, to_apply=%region_0.0 | all-reduce | flops 4096 | bytes 32768 | tf_op jit(solution)/shard_map/psum | solution.py:46
  82.9 5.8 cholesky.239
  95.0 60.6 %all-reduce.11.cloned.1.call-done = f32[64,1024]{1,0:T(8,128)} async-done(((f32[64,1024]{1,0:T(8,128)}), f32[64,1024]{1,0:T(8,128)}) %all-reduce.11.cloned.1.call-update) | async-done | bytes 262160 | tf_op jit(solution)/shard_map/psum | solution.py:53
  157.7 26.2 psum.149
  192.8 5.8 cholesky.250
  205.1 65.8 %all-reduce.13.cloned.1.call-done = f32[64,1024]{1,0:T(8,128)} async-done(((f32[64,1024]{1,0:T(8,128)}), f32[64,1024]{1,0:T(8,128)}) %all-reduce.13.cloned.1.call-update) | async-done | bytes 262160 | tf_op jit(solution)/shard_map/psum | solution.py:64
  273.0 64.9 %psum.151 = f32[64,64]{0,1:T(8,128)S(1)} all-reduce(f32[64,64]{0,1:T(8,128)S(1)} %fusion.166), channel_id=1, replica_groups=mesh['smp'=8,'bld'=16] {'bld'}, use_global_device_ids=true, to_apply=%region_10.14 | all-reduce | flops 4096 | bytes 32768 | tf_op jit(solution)/shard_map/psum | solution.py:66
  338.8 6.2 multiply_reduce_fusion.7
  345.0 176.6 %all-gather.5 = f32[128,4,64]{2,1,0:T(4,128)S(1)} all-gather(f32[1,4,64]{2,1,0:T(4,128)S(1)} %bitcast.381), channel_id=2, replica_groups=mesh['smp'=8,'bld'=16] {'smp','bld'}, dimensions={0}, use_global_device_ids=true | all-gather | bytes 132096 | tf_op jit(solution)/shard_map/all_gather | solution.py:77
  523.9 5.8 cholesky.261
  538.8 5.8 cholesky.272
  551.8 127.6 %all-reduce.15.cloned.1.call-done = f32[64,1024]{1,0:T(8,128)} async-done(((f32[64,1024]{1,0:T(8,128)}), f32[64,1024]{1,0:T(8,128)}) %all-reduce.15.cloned.1.call-update) | async-done | bytes 262160 | tf_op jit(solution)/shard_map/psum | solution.py:53
  681.5 26.5 %psum.153 = f32[64,64]{0,1:T(8,128)S(1)} all-reduce(f32[64,64]{0,1:T(8,128)S(1)} %fusion.167), channel_id=1, replica_groups=mesh['smp'=8,'bld'=16] {'smp'}, use_global_device_ids=true, to_apply=%region_17.23 | all-reduce | flops 4096 | bytes 32768 | tf_op jit(solution)/shard_map/psum | solution.py:55
  708.8 5.8 fusion.6
  716.9 5.8 cholesky.283
  729.1 65.7 %all-reduce.17.cloned.1.call-done = f32[64,1024]{1,0:T(8,128)} async-done(((f32[64,1024]{1,0:T(8,128)}), f32[64,1024]{1,0:T(8,128)}) %all-reduce.17.cloned.1.call-update) | async-done | bytes 262160 | tf_op jit(solution)/shard_map/psum | solution.py:64
  797.0 64.7 %psum.155 = f32[64,64]{0,1:T(8,128)S(1)} all-reduce(f32[64,64]{0,1:T(8,128)S(1)} %fusion.168), channel_id=1, replica_groups=mesh['smp'=8,'bld'=16] {'bld'}, use_global_device_ids=true, to_apply=%region_21.27 | all-reduce | flops 4096 | bytes 32768 | tf_op jit(solution)/shard_map/psum | solution.py:66
  862.6 6.2 multiply_reduce_fusion.5
  868.8 177.0 %all-gather.6 = f32[128,4,64]{2,1,0:T(4,128)S(1)} all-gather(f32[1,4,64]{2,1,0:T(4,128)S(1)} %bitcast.382), channel_id=3, replica_groups=mesh['smp'=8,'bld'=16] {'smp','bld'}, dimensions={0}, use_global_device_ids=true | all-gather | bytes 132096 | tf_op jit(solution)/shard_map/all_gather | solution.py:77
  1048.1 5.8 cholesky.294
  1062.9 5.8 cholesky.305
  1075.9 127.6 %all-reduce.19.cloned.1.call-done = f32[64,1024]{1,0:T(8,128)} async-done(((f32[64,1024]{1,0:T(8,128)}), f32[64,1024]{1,0:T(8,128)}) %all-reduce.19.cloned.1.call-update) | async-done | bytes 262160 | tf_op jit(solution)/shard_map/psum | solution.py:53
  1205.6 26.5 %psum.157 = f32[64,64]{0,1:T(8,128)S(1)} all-reduce(f32[64,64]{0,1:T(8,128)S(1)} %fusion.169), channel_id=1, replica_groups=mesh['smp'=8,'bld'=16] {'smp'}, use_global_device_ids=true, to_apply=%region_28.34 | all-reduce | flops 4096 | bytes 32768 | tf_op jit(solution)/shard_map/psum | solution.py:55
  1241.0 5.8 cholesky.316
  1253.3 65.4 %all-reduce.21.cloned.1.call-done = f32[64,1024]{1,0:T(8,128)} async-done(((f32[64,1024]{1,0:T(8,128)}), f32[64,1024]{1,0:T(8,128)}) %all-reduce.21.cloned.1.call-update) | async-done | bytes 262160 | tf_op jit(solution)/shard_map/psum | solution.py:64
  1320.8 64.9 %psum.159 = f32[64,64]{0,1:T(8,128)S(1)} all-reduce(f32[64,64]{0,1:T(8,128)S(1)} %fusion.170), channel_id=1, replica_groups=mesh['smp'=8,'bld'=16] {'bld'}, use_global_device_ids=true, to_apply=%region_32.38 | all-reduce | flops 4096 | bytes 32768 | tf_op jit(solution)/shard_map/psum | solution.py:66
  1386.7 6.2 multiply_reduce_fusion.3
  1392.8 176.6 %all-gather.7 = f32[128,4,64]{2,1,0:T(4,128)S(1)} all-gather(f32[1,4,64]{2,1,0:T(4,128)S(1)} %bitcast.383), channel_id=4, replica_groups=mesh['smp'=8,'bld'=16] {'smp','bld'}, dimensions={0}, use_global_device_ids=true | all-gather | bytes 132096 | tf_op jit(solution)/shard_map/all_gather | solution.py:77
  1571.7 5.8 cholesky.327
  1586.6 5.8 cholesky.338
  1599.6 127.6 %all-reduce.23.cloned.1.call-done = f32[64,1024]{1,0:T(8,128)} async-done(((f32[64,1024]{1,0:T(8,128)}), f32[64,1024]{1,0:T(8,128)}) %all-reduce.23.cloned.1.call-update) | async-done | bytes 262160 | tf_op jit(solution)/shard_map/psum | solution.py:53
  1729.3 26.5 %psum.161 = f32[64,64]{0,1:T(8,128)S(1)} all-reduce(f32[64,64]{0,1:T(8,128)S(1)} %fusion.171), channel_id=1, replica_groups=mesh['smp'=8,'bld'=16] {'smp'}, use_global_device_ids=true, to_apply=%region_39.45 | all-reduce | flops 4096 | bytes 32768 | tf_op jit(solution)/shard_map/psum | solution.py:55
  1764.7 5.8 cholesky.349
  1776.9 65.8 %all-reduce.25.cloned.1.call-done = f32[64,1024]{1,0:T(8,128)} async-done(((f32[64,1024]{1,0:T(8,128)}), f32[64,1024]{1,0:T(8,128)}) %all-reduce.25.cloned.1.call-update) | async-done | bytes 262160 | tf_op jit(solution)/shard_map/psum | solution.py:64
  1844.8 64.7 %psum.163 = f32[64,64]{0,1:T(8,128)S(1)} all-reduce(f32[64,64]{0,1:T(8,128)S(1)} %fusion.172), channel_id=1, replica_groups=mesh['smp'=8,'bld'=16] {'bld'}, use_global_device_ids=true, to_apply=%region_43.49 | all-reduce | flops 4096 | bytes 32768 | tf_op jit(solution)/shard_map/psum | solution.py:66
  1910.5 6.2 multiply_reduce_fusion.1
  1916.6 176.8 %all-gather.8 = f32[128,4,64]{2,1,0:T(4,128)S(1)} all-gather(f32[1,4,64]{2,1,0:T(4,128)S(1)} %bitcast.384), channel_id=5, replica_groups=mesh['smp'=8,'bld'=16] {'smp','bld'}, dimensions={0}, use_global_device_ids=true | all-gather | bytes 132096 | tf_op jit(solution)/shard_map/all_gather | solution.py:77
  2095.8 5.8 cholesky.360
  2110.6 5.8 cholesky.371
  2123.6 127.6 %all-reduce.27.cloned.1.call-done = f32[64,1024]{1,0:T(8,128)} async-done(((f32[64,1024]{1,0:T(8,128)}), f32[64,1024]{1,0:T(8,128)}) %all-reduce.27.cloned.1.call-update) | async-done | bytes 262160 | tf_op jit(solution)/shard_map/psum | solution.py:53
  2253.3 26.2 psum.165
  2282.7 5.8 cholesky.382
  2301.3 65.2 %all-reduce.29.cloned.1.call-done = f32[64,1024]{1,0:T(8,128)} async-done(((f32[64,1024]{1,0:T(8,128)}), f32[64,1024]{1,0:T(8,128)}) %all-reduce.29.cloned.1.call-update) | async-done | bytes 262160 | tf_op jit(solution)/shard_map/psum | solution.py:64
  2368.6 65.0 %psum.167 = f32[64,64]{0,1:T(8,128)S(1)} all-reduce(f32[64,64]{0,1:T(8,128)S(1)} %fusion.174), channel_id=1, replica_groups=mesh['smp'=8,'bld'=16] {'bld'}, use_global_device_ids=true, to_apply=%region_54.60 | all-reduce | flops 4096 | bytes 32768 | tf_op jit(solution)/shard_map/psum | solution.py:66
  2434.6 6.1 fusion.11
  2440.8 176.6 %all-gather.9 = f32[128,4,64]{2,1,0:T(4,128)S(1)} all-gather(f32[1,4,64]{2,1,0:T(4,128)S(1)} %bitcast.380), channel_id=6, replica_groups=mesh['smp'=8,'bld'=16] {'smp','bld'}, dimensions={0}, use_global_device_ids=true | all-gather | bytes 132096 | tf_op jit(solution)/shard_map/all_gather | solution.py:77
  2619.7 5.8 cholesky.393
  (258 shorter events, 180.0 us)
Async XLA Ops:
  7.2 73.3 %copy-start.1 = (f32[4,64]{1,0:T(4,128)S(1)}, f32[4,64]{1,0:T(4,128)}, u32[]{:S(2)}) copy-start(f32[4,64]{1,0:T(4,128)} %param.14) | copy-start | bytes 3076
  7.2 7.6 copy-start
  7.2 148.4 %all-reduce.11.cloned.1.call-start = ((), (), s32[]{:S(2)}) async-start(), calls=%async_computation | async-start | bytes 524288 | tf_op jit(solution)/shard_map/psum | solution.py:53
  14.7 256.2 %all-reduce.13.cloned.1.call-start = ((), (), s32[]{:S(2)}) async-start(), calls=%async_computation.1 | async-start | bytes 524288 | tf_op jit(solution)/shard_map/psum | solution.py:64
  199.4 480.0 %all-reduce.15.cloned.1.call-start = ((), (), s32[]{:S(2)}) async-start(), calls=%async_computation.2 | async-start | bytes 524288 | tf_op jit(solution)/shard_map/psum | solution.py:53
  545.5 249.4 %all-reduce.17.cloned.1.call-start = ((), (), s32[]{:S(2)}) async-start(), calls=%async_computation.3 | async-start | bytes 524288 | tf_op jit(solution)/shard_map/psum | solution.py:64
  723.4 480.1 %all-reduce.19.cloned.1.call-start = ((), (), s32[]{:S(2)}) async-start(), calls=%async_computation.4 | async-start | bytes 524288 | tf_op jit(solution)/shard_map/psum | solution.py:53
  1069.7 249.0 %all-reduce.21.cloned.1.call-start = ((), (), s32[]{:S(2)}) async-start(), calls=%async_computation.5 | async-start | bytes 524288 | tf_op jit(solution)/shard_map/psum | solution.py:64
  1247.6 479.6 %all-reduce.23.cloned.1.call-start = ((), (), s32[]{:S(2)}) async-start(), calls=%async_computation.6 | async-start | bytes 524288 | tf_op jit(solution)/shard_map/psum | solution.py:53
  1593.3 249.4 %all-reduce.25.cloned.1.call-start = ((), (), s32[]{:S(2)}) async-start(), calls=%async_computation.7 | async-start | bytes 524288 | tf_op jit(solution)/shard_map/psum | solution.py:64
  1771.2 480.0 %all-reduce.27.cloned.1.call-start = ((), (), s32[]{:S(2)}) async-start(), calls=%async_computation.8 | async-start | bytes 524288 | tf_op jit(solution)/shard_map/psum | solution.py:53
  2117.4 249.1 %all-reduce.29.cloned.1.call-start = ((), (), s32[]{:S(2)}) async-start(), calls=%async_computation.9 | async-start | bytes 524288 | tf_op jit(solution)/shard_map/psum | solution.py:64
Sparse Core Ops, SparseCore 0:
  14.8 140.7 all-reduce.10
  199.5 71.3 all-reduce.12
  545.6 133.6 all-reduce.14
  723.5 71.2 all-reduce.16
  1069.8 133.6 all-reduce.18
  1247.7 70.9 all-reduce.20
  1593.5 133.6 all-reduce.22
  1771.3 71.3 all-reduce.24
  2117.5 133.6 all-reduce.26
  2295.1 71.3 all-reduce.28
